TPU v7x, 32 devices: a whole 2x2x4 slice. The times are simulated.
32 devices in a mesh: grp: 4 (over y, x), leaf: 8 (over z, core).
Axes of the slice: x: 2, y: 2, z: 4, core: 2. Of those that a mesh axis runs over, the one named last changes fastest.
Arguments:
- basis: float32 [8, 65536], P(None, ('grp', 'leaf')), may hold values from -28 to 28
- roots: float32 [5], replicated, may hold values from 0.35 to 1
- near_blocks: bfloat16 [256, 6, 256, 256], P(('grp', 'leaf')), may hold values from -0.046875 to 0.046875
- near_ids: int32 [256, 6], P(('grp', 'leaf')), may hold values from 0 to 255, as said below
- leaf_basis: bfloat16 [256, 64, 256], P(('grp', 'leaf')), may hold values from -0.375 to 0.375
- far_coupling: bfloat16 [256, 8, 64, 64], P(('grp', 'leaf')), may hold values from -0.109375 to 0.109375
- far_ids: int32 [256, 8], P(('grp', 'leaf')), may hold values from 0 to 255, as said below
- transfer: bfloat16 [256, 64, 128], P(('grp', 'leaf')), may hold values from -0.5 to 0.5
- top_coupling: bfloat16 [128, 8, 128, 128], P(('grp', 'leaf')), may hold values from -0.078125 to 0.078125
- top_ids: int32 [128, 8], P(('grp', 'leaf')), may hold values from 0 to 127, as said below
Outputs:
- next_vector: float32 [65536], P(('grp', 'leaf'))
- hessen: float32 [9], replicated
Inputs may be any that keep to these rules, and one draw needn't show every extreme that they name: `near_ids`: row i starts with i itself; the others lie within 8 leaves of i. `far_ids`: every entry lies within 8 leaves of its row. `top_ids`: every entry lies within 4 parents of its row.
All inputs are finite; a program needn't handle non-finite values.
Results may differ from a plain program's by a relative error of at most 0.024.
Values may be sent and summed in bfloat16 or wider, within the bound.
A program may use at most 64 MiB of HBM per device.

v0:
```python
import functools

import jax
import jax.numpy as jnp
from jax import lax
from jax.experimental import pallas as pl
from jax.experimental.pallas import tpu as pltpu
from jax.sharding import PartitionSpec as P

MESH = pl.DeviceIdType.MESH
F32 = jnp.float32
BF16 = jnp.bfloat16


def nt(a, b):
    return lax.dot_general(a, b, (((1,), (1,)), ((), ())), preferred_element_type=F32)


def nn(a, b):
    return lax.dot_general(a, b, (((1,), (0,)), ((), ())), preferred_element_type=F32)


def kernel(
    n_grp,
    n_leaf,
    basis,
    roots,
    near_hbm,
    near_ids,
    lb_hbm,
    fc_hbm,
    far_ids,
    tr_hbm,
    tc_hbm,
    top_ids,
    out,
    hess,
    near,
    lb,
    fc,
    fcc,
    tr,
    tc,
    halo,
    prod_buf,
    z_buf,
    slots,
    load_sem,
    near_sem,
    send_sem,
    recv_sem,
    red_sem,
):
    n_dev = n_grp * n_leaf
    count = basis.shape[0]
    leaves, n_near, width, _ = near.shape
    n_far, rank = fc.shape[1], fc.shape[2]
    n_top, prank = tc.shape[1], tc.shape[2]
    parents = tc.shape[0]
    steps = roots.shape[0]
    coefs = leaves * rank
    me = lax.axis_index("grp") * n_leaf + lax.axis_index("leaf")

    def place(index):
        return (index // n_leaf, index % n_leaf)

    right = lax.rem(me + 1, n_dev)
    left = lax.rem(me + n_dev - 1, n_dev)

    lb_copy = pltpu.make_async_copy(lb_hbm, lb, load_sem.at[0])
    tr_copy = pltpu.make_async_copy(tr_hbm, tr, load_sem.at[1])
    fc_copy = pltpu.make_async_copy(fc_hbm, fc, load_sem.at[2])
    tc_copy = pltpu.make_async_copy(tc_hbm, tc, load_sem.at[3])
    near_copies = [
        pltpu.make_async_copy(near_hbm.at[i], near.at[i], near_sem.at[i]) for i in range(leaves)
    ]
    lb_copy.start()
    tr_copy.start()
    fc_copy.start()
    tc_copy.start()
    for copy in near_copies:
        copy.start()

    barrier = pltpu.get_barrier_semaphore()

    def greet(d, carry):
        pl.semaphore_signal(
            barrier, inc=1, device_id=place(lax.rem(me + d, n_dev)), device_id_type=MESH
        )
        return carry

    lax.fori_loop(1, n_dev, greet, 0)

    for i in range(leaves):
        prod_buf[i : i + 1, :] = basis[count - 1 : count, i * width : (i + 1) * width]
    z_buf[...] = jnp.zeros_like(z_buf)

    def iota(shape, dim):
        return lax.broadcasted_iota(jnp.int32, shape, dim)

    cands = 4 * leaves

    def onehots(columns):
        return [jnp.where(c == iota((leaves, cands), 1), 1.0, 0.0).astype(F32) for c in columns]

    base = me * leaves - leaves
    nid = near_ids[...] - base
    near_hot = jnp.concatenate(onehots([nid[:, k : k + 1] for k in range(1, n_near)]), 0)
    near_hot = near_hot.astype(BF16)
    fid = far_ids[...] - base
    far_hot = jnp.concatenate(onehots([fid[:, k : k + 1] for k in range(n_far)]), 0).astype(BF16)
    base_p = me * parents - parents
    tid = jnp.zeros((leaves, n_top), jnp.int32)
    for p in range(parents):
        tid = jnp.where(iota((leaves, n_top), 0) // 2 == p, top_ids[p : p + 1, :], tid)
    tid = (tid - base_p) * 2
    top_hot = jnp.concatenate(onehots([tid[:, k : k + 1] for k in range(n_top)]), 0).astype(BF16)

    gram = lax.dot_general(
        basis[...],
        basis[...],
        (((1,), (1,)), ((), ())),
        precision=lax.Precision.HIGHEST,
        preferred_element_type=F32,
    )

    row512 = iota((leaves, coefs), 0)
    block512 = iota((leaves, coefs), 1) // rank
    diag = row512 == block512
    row_l = iota((leaves, 2 * rank), 0)
    row_w = iota((leaves, width), 0)
    row_p = iota((leaves, prank), 0)
    low = iota((leaves, 2 * rank), 1) < rank

    fc_copy.wait()
    for k in range(n_far):
        for i in range(leaves):
            fcc[i * rank : (i + 1) * rank, k * rank : (k + 1) * rank] = fc[i, k]
    lb_copy.wait()
    tr_copy.wait()
    pl.semaphore_wait(barrier, n_dev - 1)

    def apply(step, field, first):
        xb = field.astype(BF16)
        full = jnp.where(diag, nt(xb, lb[...]), 0.0)
        part = full[:, 0 : 2 * rank]
        for v in range(1, leaves // 2):
            part = part + full[:, v * 2 * rank : (v + 1) * 2 * rank]
        part = part.astype(BF16).astype(F32)
        dup = part + pltpu.roll(part, rank, 1)
        swapped = jnp.where(
            row_l % 2 == 0, pltpu.roll(part, leaves - 1, 0), pltpu.roll(part, 1, 0)
        )
        pair = part + swapped
        lhs = jnp.concatenate(
            [jnp.where(row_l // 2 == v, pair, 0.0) for v in range(leaves // 2)], 1
        ).astype(BF16)
        up = nn(lhs, tr[...]).astype(BF16).astype(F32)
        halo[step, 1, :, 0:width] = xb.astype(F32)
        halo[step, 1, :, width : width + 2 * rank] = dup
        halo[step, 1, :, width + 2 * rank :] = up
        copies = []
        for side, target in ((0, right), (2, left)):
            copy = pltpu.make_async_remote_copy(
                src_ref=halo.at[step, 1],
                dst_ref=halo.at[step, side],
                send_sem=send_sem.at[step, side // 2],
                recv_sem=recv_sem.at[step, side // 2],
                device_id=place(target),
                device_id_type=MESH,
            )
            copy.start()
            copies.append(copy)
        acc = 0.5 * field
        own = []
        for i in range(leaves):
            if first:
                near_copies[i].wait()
            own.append(nt(xb, near[i, 0]))
        if first:
            tc_copy.wait()
        for copy in copies:
            copy.wait()
        cand = jnp.concatenate(
            [halo[step, 0], halo[step, 1], halo[step, 2], jnp.zeros_like(halo[step, 0])], 0
        ).astype(BF16)
        coef = nn(far_hot, cand[:, width : width + 2 * rank])
        par = nn(top_hot, cand[:, width + 2 * rank :])
        near_x = nn(near_hot, cand[:, 0:width])
        par_k = [par[k * leaves : (k + 1) * leaves].astype(BF16) for k in range(n_top)]
        srow = jnp.zeros((leaves, prank), F32)
        for p in range(parents):
            r = nt(par_k[0], tc[p, 0])
            for k in range(1, n_top):
                r = r + nt(par_k[k], tc[p, k])
            srow = jnp.where(row_p // 2 == p, r, srow)
        far_lhs = jnp.concatenate(
            [
                jnp.where(
                    low,
                    coef[2 * v * leaves : (2 * v + 1) * leaves],
                    coef[(2 * v + 1) * leaves : (2 * v + 2) * leaves],
                )
                for v in range(n_far // 2)
            ],
            1,
        ).astype(BF16)
        leaf_sum = nt(far_lhs, fcc[...])
        down = nt(srow.astype(BF16), tr[...])
        g = jnp.where(diag, leaf_sum + down, 0.0).astype(BF16)
        far = nn(g, lb[...])
        acc = acc + far
        xk = [near_x[k * leaves : (k + 1) * leaves].astype(BF16) for k in range(n_near - 1)]
        for i in range(leaves):
            r = own[i]
            for k in range(1, n_near):
                r = r + nt(xk[k - 1], near[i, k])
            acc = acc + jnp.where(row_w == i, r, 0.0)
        return acc

    def body(step, first):
        root = roots[step]
        prod = prod_buf[...]
        scaled = prod / root
        z = z_buf[...] + scaled
        z_buf[...] = z
        last = step == steps - 1
        field = jnp.where(last, z, prod)
        image = apply(step, field, first)
        prod_buf[...] = jnp.where(last, image, prod - image / root)

    body(0, True)

    def loop(step, carry):
        body(step, False)
        return carry

    lax.fori_loop(1, steps, loop, 0)

    w = prod_buf[...]
    proj = jnp.zeros((count, width), F32)
    for i in range(leaves):
        proj = proj + basis[:, i * width : (i + 1) * width] * w[i : i + 1, :]
    hcol = jnp.sum(proj, 1, keepdims=True)
    wcol = jnp.sum(w * w, 1, keepdims=True)
    lane = iota((count, 128), 1)
    rows = iota((count, 128), 0)
    tile = jnp.where(lane == count, hcol, 0.0) + jnp.where(lane == count + 1, wcol, 0.0)
    tile = tile + jnp.pad(gram, ((0, 0), (0, 128 - count)))
    slots[me] = tile

    def spread(d, carry):
        pltpu.make_async_remote_copy(
            src_ref=slots.at[me],
            dst_ref=slots.at[me],
            send_sem=red_sem.at[0],
            recv_sem=red_sem.at[1],
            device_id=place(lax.rem(me + d, n_dev)),
            device_id_type=MESH,
        ).start()
        return carry

    lax.fori_loop(1, n_dev, spread, 0)
    rest = pltpu.make_async_remote_copy(
        src_ref=slots.at[pl.ds(0, n_dev - 1)],
        dst_ref=slots.at[pl.ds(0, n_dev - 1)],
        send_sem=red_sem.at[0],
        recv_sem=red_sem.at[1],
        device_id=place(right),
        device_id_type=MESH,
    )
    rest.wait_recv()
    total = jnp.sum(slots[...], 0) * (1.0 / (leaves * width * n_dev))
    h = jnp.sum(jnp.where(lane == count, total, 0.0), 1, keepdims=True)
    ww = jnp.sum(jnp.where(lane == count + 1, total, 0.0), keepdims=True)
    hrow = jnp.sum(jnp.where(lane == rows, h, 0.0), 0, keepdims=True)
    quad = jnp.sum(h * (total * hrow), keepdims=True)
    hh = jnp.sum(h * h, keepdims=True)
    squared = jnp.maximum(ww - 2.0 * hh + quad, 0.0)
    beta = jnp.sqrt(squared + 1e-06)
    inverse = 1.0 / beta
    lane1 = iota((1, 128), 1)
    full = jnp.where(lane1 == count, beta, hrow)
    hess[...] = full[:, 0 : count + 1]
    for i in range(leaves):
        fit = jnp.sum(basis[:, i * width : (i + 1) * width] * h, 0, keepdims=True)
        out[:, i * width : (i + 1) * width] = (w[i : i + 1, :] - fit) * inverse
    rest.wait_send()


def make_body(n_grp, n_leaf):
    def body(
        basis,
        roots,
        near_blocks,
        near_ids,
        leaf_basis,
        far_coupling,
        far_ids,
        transfer,
        top_coupling,
        top_ids,
    ):
        leaves, rank, width = leaf_basis.shape
        prank = transfer.shape[2]
        count = basis.shape[0]
        steps = roots.shape[0]
        n_dev = n_grp * n_leaf
        payload = width + 2 * rank + prank
        vmem = pl.BlockSpec(memory_space=pltpu.VMEM)
        smem = pl.BlockSpec(memory_space=pltpu.SMEM)
        hbm = pl.BlockSpec(memory_space=pl.ANY)
        lb = leaf_basis.reshape(leaves * rank, width)
        tr = transfer.reshape(leaves * rank, prank)
        n_far = far_coupling.shape[1]
        out, hess = pl.pallas_call(
            functools.partial(kernel, n_grp, n_leaf),
            out_shape=(
                jax.ShapeDtypeStruct((1, leaves * width), F32),
                jax.ShapeDtypeStruct((1, count + 1), F32),
            ),
            in_specs=[vmem, smem, hbm, vmem, hbm, hbm, vmem, hbm, hbm, vmem],
            out_specs=(vmem, vmem),
            scratch_shapes=[
                pltpu.VMEM(near_blocks.shape, BF16),
                pltpu.VMEM(lb.shape, BF16),
                pltpu.VMEM(far_coupling.shape, BF16),
                pltpu.VMEM((leaves * rank, n_far * rank), BF16),
                pltpu.VMEM(tr.shape, BF16),
                pltpu.VMEM(top_coupling.shape, BF16),
                pltpu.VMEM((steps, 3, leaves, payload), F32),
                pltpu.VMEM((leaves, width), F32),
                pltpu.VMEM((leaves, width), F32),
                pltpu.VMEM((n_dev, count, 128), F32),
                pltpu.SemaphoreType.DMA((4,)),
                pltpu.SemaphoreType.DMA((leaves,)),
                pltpu.SemaphoreType.DMA((steps, 2)),
                pltpu.SemaphoreType.DMA((steps, 2)),
                pltpu.SemaphoreType.DMA((2,)),
            ],
            compiler_params=pltpu.CompilerParams(
                collective_id=0, has_side_effects=True, vmem_limit_bytes=48 * 1024 * 1024
            ),
        )(
            basis,
            roots,
            near_blocks,
            near_ids,
            lb,
            far_coupling,
            far_ids,
            tr,
            top_coupling,
            top_ids,
        )
        return out.reshape(leaves * width), hess.reshape(count + 1)

    return body


def solution(mesh):
    both = ("grp", "leaf")
    return jax.shard_map(
        make_body(mesh.shape["grp"], mesh.shape["leaf"]),
        mesh=mesh,
        in_specs=(
            P(None, both),
            P(),
            P(both, None, None, None),
            P(both, None),
            P(both, None, None),
            P(both, None, None, None),
            P(both, None),
            P(both, None, None),
            P(both, None, None, None),
            P(both, None),
        ),
        out_specs=(P(both), P()),
        check_vma=False,
    )
```

profile of v0, /device:TPU:0, one launch (start us, length us, event | category | flops | bytes accessed | tf_op | source)
XLA Modules:
  0.0 58.0 jit_solution(1529397592560789706)
XLA Ops:
  0.6 0.0 copy-start
  0.6 1.2 %copy-done = bf16[8,8,64,64]{3,2,1,0:T(8,128)(2,1)S(1)} copy-done((bf16[8,8,64,64]{3,2,1,0:T(8,128)(2,1)S(1)}, bf16[8,8,64,64]{3,2,1,0:T(8,128)(2,1)}, u32[]{:S(2)}) %copy-start) | copy-done | bytes 524312
  1.9 0.0 copy-start.1
  1.9 1.2 %copy-done.1 = bf16[4,8,128,128]{3,2,1,0:T(8,128)(2,1)S(1)} copy-done((bf16[4,8,128,128]{3,2,1,0:T(8,128)(2,1)S(1)}, bf16[4,8,128,128]{3,2,1,0:T(8,128)(2,1)}, u32[]{:S(2)}) %copy-start.1) | copy-done | bytes 1048600
  3.1 0.0 copy-start.2
  3.1 0.9 %copy-done.2 = bf16[8,64,256]{2,1,0:T(8,128)(2,1)S(1)} copy-done((bf16[8,64,256]{2,1,0:T(8,128)(2,1)S(1)}, bf16[8,64,256]{2,1,0:T(8,128)(2,1)}, u32[]{:S(2)}) %copy-start.2) | copy-done | bytes 262168
  4.0 0.0 copy-start.3
  4.0 0.9 %copy-done.3 = bf16[8,64,128]{2,1,0:T(8,128)(2,1)S(1)} copy-done((bf16[8,64,128]{2,1,0:T(8,128)(2,1)S(1)}, bf16[8,64,128]{2,1,0:T(8,128)(2,1)}, u32[]{:S(2)}) %copy-start.3) | copy-done | bytes 131096
  4.9 0.0 copy-start.4
  4.9 0.8 %copy-done.4 = f32[8,2048]{1,0:T(8,128)S(1)} copy-done((f32[8,2048]{1,0:T(8,128)S(1)}, f32[8,2048]{1,0:T(8,128)}, u32[]{:S(2)}) %copy-start.4) | copy-done | bytes 65560
  5.8 0.0 copy-start.5
  5.8 0.7 %copy-done.5 = s32[8,6]{1,0:T(8,128)S(1)} copy-done((s32[8,6]{1,0:T(8,128)S(1)}, s32[8,6]{1,0:T(8,128)}, u32[]{:S(2)}) %copy-start.5) | copy-done | bytes 216
  6.5 0.0 copy-start.6
  6.5 0.7 %copy-done.6 = s32[8,8]{1,0:T(8,128)S(1)} copy-done((s32[8,8]{1,0:T(8,128)S(1)}, s32[8,8]{1,0:T(8,128)}, u32[]{:S(2)}) %copy-start.6) | copy-done | bytes 280
  7.2 0.0 copy-start.7
  7.2 0.7 %copy-done.7 = s32[4,8]{1,0:T(4,128)S(1)} copy-done((s32[4,8]{1,0:T(4,128)S(1)}, s32[4,8]{1,0:T(4,128)}, u32[]{:S(2)}) %copy-start.7) | copy-done | bytes 152
  7.8 0.0 copy-start.8
  7.8 0.7 %copy-done.8 = f32[5]{0:T(128)S(1)} copy-done((f32[5]{0:T(128)S(1)}, f32[5]{0:T(128)}, u32[]{:S(2)}) %copy-start.8) | copy-done | bytes 44
  8.5 48.4 %shard_map.113 = (f32[1,2048]{1,0:T(1,128)S(1)}, f32[1,9]{1,0:T(1,128)S(1)}) custom-call(f32[8,2048]{1,0:T(8,128)S(1)} %copy-done.4, f32[5]{0:T(128)S(1)} %copy-done.8, bf16[8,6,256,256]{3,2,1,0:T(8,128)(2,1)} %near_hbm.1, s32[8,6]{1,0:T(8,128)S(1)} %copy-done.5, bf16[512,256]{1,0:T(8,128)(2,1)S(1)} %bitcast.4, bf16[8,8,64,64]{3,2,1,0:T(8,128)(2,1)S(1)} %copy-done, ...), custom_call_target="tpu_custom_call" | custom-call | tf_op jit(solution)/shard_map/pallas_call | solution.py:316
  56.9 0.6 %copy.14 = f32[2048]{0:T(1024)} copy(f32[2048]{0:T(1024)S(1)} %bitcast.6) | data formatting | bytes 16384
  57.5 0.5 copy.15
Async XLA Ops:
  0.6 1.2 %copy-start = (bf16[8,8,64,64]{3,2,1,0:T(8,128)(2,1)S(1)}, bf16[8,8,64,64]{3,2,1,0:T(8,128)(2,1)}, u32[]{:S(2)}) copy-start(bf16[8,8,64,64]{3,2,1,0:T(8,128)(2,1)} %fc_hbm.1) | copy-start | bytes 1572868
  1.9 1.2 %copy-start.1 = (bf16[4,8,128,128]{3,2,1,0:T(8,128)(2,1)S(1)}, bf16[4,8,128,128]{3,2,1,0:T(8,128)(2,1)}, u32[]{:S(2)}) copy-start(bf16[4,8,128,128]{3,2,1,0:T(8,128)(2,1)} %tc_hbm.1) | copy-start | bytes 3145732
  3.1 0.9 %copy-start.2 = (bf16[8,64,256]{2,1,0:T(8,128)(2,1)S(1)}, bf16[8,64,256]{2,1,0:T(8,128)(2,1)}, u32[]{:S(2)}) copy-start(bf16[8,64,256]{2,1,0:T(8,128)(2,1)} %param.14) | copy-start | bytes 786436
  4.0 0.9 %copy-start.3 = (bf16[8,64,128]{2,1,0:T(8,128)(2,1)S(1)}, bf16[8,64,128]{2,1,0:T(8,128)(2,1)}, u32[]{:S(2)}) copy-start(bf16[8,64,128]{2,1,0:T(8,128)(2,1)} %param.17) | copy-start | bytes 393220
  4.9 0.8 %copy-start.4 = (f32[8,2048]{1,0:T(8,128)S(1)}, f32[8,2048]{1,0:T(8,128)}, u32[]{:S(2)}) copy-start(f32[8,2048]{1,0:T(8,128)} %basis.1) | copy-start | bytes 196612
  5.8 0.7 %copy-start.5 = (s32[8,6]{1,0:T(8,128)S(1)}, s32[8,6]{1,0:T(8,128)}, u32[]{:S(2)}) copy-start(s32[8,6]{1,0:T(8,128)} %near_ids.1) | copy-start | bytes 580
  6.5 0.7 %copy-start.6 = (s32[8,8]{1,0:T(8,128)S(1)}, s32[8,8]{1,0:T(8,128)}, u32[]{:S(2)}) copy-start(s32[8,8]{1,0:T(8,128)} %far_ids.1) | copy-start | bytes 772
  7.2 0.7 %copy-start.7 = (s32[4,8]{1,0:T(4,128)S(1)}, s32[4,8]{1,0:T(4,128)}, u32[]{:S(2)}) copy-start(s32[4,8]{1,0:T(4,128)} %top_ids.1) | copy-start | bytes 388
  7.8 0.7 %copy-start.8 = (f32[5]{0:T(128)S(1)}, f32[5]{0:T(128)}, u32[]{:S(2)}) copy-start(f32[5]{0:T(128)} %roots.1) | copy-start | bytes 64
where the time goes:
time: 58.4 us; the launch traced here: 58 us
  Pallas kernels  48.4 us (83%)
  local copies, waits for them, and re-layouts  8.95 us (15%)
  between operations  0.66 us (1%)
    pallas_call x1, Pallas kernels, body(): pl.pallas_call(functools.partial(kernel, n_grp, n_leaf), out_shape=(jax.S...  48.4 us
    unnamed x20, local copies, waits for them, and re-layouts  8.95 us

commit v1 on v0

v1 whole, which is shorter than its diff:
```python
import functools

import jax
import jax.numpy as jnp
from jax import lax
from jax.experimental import pallas as pl
from jax.experimental.pallas import tpu as pltpu
from jax.sharding import PartitionSpec as P

MESH = pl.DeviceIdType.MESH
F32 = jnp.float32
BF16 = jnp.bfloat16
LANES = 128


def nt(a, b):
    return lax.dot_general(a, b, (((1,), (1,)), ((), ())), preferred_element_type=F32)


def nn(a, b):
    return lax.dot_general(a, b, (((1,), (0,)), ((), ())), preferred_element_type=F32)


def iota(shape, dim):
    return lax.broadcasted_iota(jnp.int32, shape, dim)


def kernel(
    n_grp,
    n_leaf,
    basis_hbm,
    roots_hbm,
    near_hbm,
    near_ids_hbm,
    lb_hbm,
    fc_hbm,
    far_ids_hbm,
    tr_hbm,
    tc_hbm,
    top_ids_hbm,
    out,
    hess,
    bas,
    roots,
    near,
    near_t,
    near_ids,
    lb,
    up_w,
    fc,
    fcc,
    far_ids,
    tr,
    tc,
    top_ids,
    g_w,
    near_ix,
    far_ix,
    top_ix,
    own_x,
    own_ct,
    halo_x,
    halo_ct,
    prod_buf,
    z_buf,
    w_buf,
    gram_row,
    slots,
    load_sem,
    near_sem,
    send_sem,
    recv_sem,
    red_sem,
):
    n_dev = n_grp * n_leaf
    leaves, n_near, width, _ = near.shape
    n_far, rank = fc.shape[1], fc.shape[2]
    n_top, prank = tc.shape[1], tc.shape[2]
    parents = tc.shape[0]
    count = basis_hbm.shape[0]
    steps = roots.shape[1]
    coefs = leaves * rank
    halves = width // LANES
    chunks = leaves * halves
    far_tiles = n_far * rank // LANES
    mg, ml = lax.axis_index("grp"), lax.axis_index("leaf")
    me = mg * n_leaf + ml

    def place(index):
        return (lax.div(index, n_leaf), lax.rem(index, n_leaf))

    odd = lax.rem(me, 2)
    fast = me + 1 - 2 * odd
    slow = me - 1 + 2 * odd
    has_slow = jnp.logical_and(slow >= 0, slow < n_dev)

    def others():
        for dg in range(n_grp):
            g = lax.rem(mg + dg, n_grp)
            for dl in range(n_leaf):
                if dg or dl:
                    yield (g, lax.rem(ml + dl, n_leaf))

    first = [
        pltpu.make_async_copy(
            basis_hbm.at[:, c * LANES : (c + 1) * LANES],
            bas.at[c * count : (c + 1) * count, :],
            load_sem.at[0],
        )
        for c in range(chunks)
    ]
    all_basis = pltpu.make_async_copy(bas, bas, load_sem.at[0])
    loads = [
        pltpu.make_async_copy(src, dst, load_sem.at[1 + n])
        for n, (src, dst) in enumerate(
            (
                (roots_hbm, roots),
                (near_ids_hbm, near_ids),
                (far_ids_hbm, far_ids),
                (top_ids_hbm, top_ids),
                (lb_hbm, lb),
                (tr_hbm, tr),
                (fc_hbm, fc),
                (tc_hbm, tc),
            )
        )
    ]
    lb_copy, tr_copy, fc_copy, tc_copy = loads[4:]
    for copy in first + loads:
        copy.start()
    for i in range(leaves):
        pltpu.make_async_copy(near_hbm.at[i], near.at[i], near_sem.at[i]).start()

    barrier = pltpu.get_barrier_semaphore()
    for target in others():
        pl.semaphore_signal(barrier, inc=1, device_id=target, device_id_type=MESH)

    row = iota((leaves, LANES), 0)
    lane = iota((leaves, LANES), 1)
    low = lane < rank
    even = row % 2 == 0
    own_base = me * leaves
    shift = (1 - 2 * odd) * leaves

    def side_tile(source, j, lo):
        return jnp.broadcast_to(source[j : j + 1, lo : lo + LANES], (leaves, LANES))

    @pl.when(jnp.logical_not(has_slow))
    def _():
        for step in range(steps):
            halo_x[step, 1] = jnp.zeros((leaves, width), F32)
            halo_ct[step, 1] = jnp.zeros((2 * leaves, LANES), F32)

    for copy in loads[:4]:
        copy.wait()
    nid = near_ids[...] - own_base
    for k in range(1, n_near):
        tile = jnp.broadcast_to(nid[:, k : k + 1], (leaves, LANES))
        near_ix[0, k - 1] = tile
        near_ix[1, k - 1] = tile - shift
        near_ix[2, k - 1] = tile + shift
    fid = far_ids[...] - own_base
    for v in range(far_tiles):
        tile = jnp.where(low, fid[:, 2 * v : 2 * v + 1], fid[:, 2 * v + 1 : 2 * v + 2])
        far_ix[0, v] = tile
        far_ix[1, v] = tile - shift
        far_ix[2, v] = tile + shift
    tid = jnp.zeros((leaves, n_top), jnp.int32)
    for p in range(parents):
        tid = jnp.where(iota((leaves, n_top), 0) // 2 == p, top_ids[p : p + 1, :], tid)
    tid = (tid - me * parents) * 2
    for k in range(n_top):
        tile = jnp.broadcast_to(tid[:, k : k + 1], (leaves, LANES))
        top_ix[0, k] = tile
        top_ix[1, k] = tile - shift
        top_ix[2, k] = tile + shift

    all_basis.wait()
    for h in range(halves):
        prod_buf[:, h * LANES : (h + 1) * LANES] = bas[
            pl.ds(count - 1 + count * h, leaves, stride=count * halves), :
        ]
    z_buf[...] = jnp.zeros_like(z_buf)

    lb_copy.wait()
    lb_t = lb[...].T
    up_w[:, 0:coefs] = lb_t
    tr_copy.wait()
    for i in range(leaves):
        block = nn(lb_t[:, i * rank : (i + 1) * rank], tr[i * rank : (i + 1) * rank, :])
        up_w[:, coefs + i * prank : coefs + (i + 1) * prank] = block.astype(BF16)

    pl.semaphore_wait(barrier, n_dev - 1)

    def x_copy(step, side):
        return pltpu.make_async_remote_copy(
            src_ref=own_x.at[step],
            dst_ref=halo_x.at[step, side],
            send_sem=send_sem.at[step, 0, side],
            recv_sem=recv_sem.at[step, 0, side],
            device_id=place((fast, slow)[side]),
            device_id_type=MESH,
        )

    def ct_copy(step, side):
        return pltpu.make_async_remote_copy(
            src_ref=own_ct.at[step],
            dst_ref=halo_ct.at[step, side],
            send_sem=send_sem.at[step, 1, side],
            recv_sem=recv_sem.at[step, 1, side],
            device_id=place((fast, slow)[side]),
            device_id_type=MESH,
        )

    def send(step, make):
        @pl.when(has_slow)
        def _():
            make(step, 1).start()

        make(step, 0).start()

    def receive(step, make, side):
        if side == 0:
            make(step, 0).wait_recv()
        else:

            @pl.when(has_slow)
            def _():
                make(step, 1).wait_recv()

    def pick_x(ix, source, acc):
        out = [list(a) for a in acc]
        rows = [[side_tile(source, j, h * LANES) for h in range(halves)] for j in range(leaves)]
        for k in range(n_near - 1):
            index = near_ix[ix, k]
            for j in range(leaves):
                hit = index == j
                for h in range(halves):
                    out[k][h] = jnp.where(hit, rows[j][h], out[k][h])
        return out

    def pick_ct(ix, source, far, top):
        far, top = list(far), list(top)
        for j in range(leaves):
            tile = side_tile(source, j, 0)
            for v in range(far_tiles):
                far[v] = jnp.where(far_ix[ix, v] == j, tile, far[v])
        for j in range(0, leaves, 2):
            tile = side_tile(source, leaves + j, 0)
            for k in range(n_top):
                top[k] = jnp.where(top_ix[ix, k] == j, tile, top[k])
        return far, top

    def prepare():
        def turn(i, carry):
            pltpu.make_async_copy(near_hbm.at[i], near.at[i], near_sem.at[i]).wait()
            for k in range(n_near):
                near_t[i, k] = near[i, k].T
            return carry

        lax.fori_loop(0, leaves, turn, 0)
        fc_copy.wait()
        for k in range(n_far):
            for i in range(leaves):
                fcc[i * rank : (i + 1) * rank, k * rank : (k + 1) * rank] = fc[i, k]
        g_w[0 : n_far * rank, :] = fcc[...].T
        tc_copy.wait()
        base = n_far * rank

        def fold(k, carry):
            start = pl.multiple_of(base + k * prank, prank)
            for p in range(parents):
                pair = tr[p * 2 * rank : (p + 1) * 2 * rank, :]
                block = nn(pair, tc[p, k]).astype(BF16).T
                g_w[pl.ds(start, prank), p * 2 * rank : (p + 1) * 2 * rank] = block
            return carry

        lax.fori_loop(0, n_top, fold, 0)
        flat = jnp.concatenate(
            [bas[c * count : (c + 1) * count, :] for c in range(chunks)], 1
        )
        gram = lax.dot_general(
            flat,
            flat,
            (((1,), (1,)), ((), ())),
            precision=lax.Precision.HIGHEST,
            preferred_element_type=F32,
        )
        flip = iota((count, count), 0) + iota((count, count), 1) == count - 1
        gram = lax.dot_general(
            flip.astype(F32),
            gram,
            (((1,), (0,)), ((), ())),
            precision=lax.Precision.HIGHEST,
            preferred_element_type=F32,
        )
        gram = jnp.pad(gram, ((0, 0), (0, LANES - count)))
        spread = pltpu.roll(gram, 0, 1, stride=count, stride_axis=0)
        gram_row[...] = jnp.sum(spread, 0, keepdims=True)

    diag = iota((leaves, coefs), 0) == iota((leaves, coefs), 1) // rank
    row_w = iota((leaves, width), 0)

    def apply(step, field, early):
        own_x[step] = field
        send(step, x_copy)
        xb = field.astype(BF16)
        full = nn(xb, up_w[...])
        masked = jnp.where(diag, full[:, 0:coefs], 0.0)
        part = masked[:, 0:LANES]
        for v in range(1, coefs // LANES):
            part = part + masked[:, v * LANES : (v + 1) * LANES]
        dup = part + pltpu.roll(part, rank, 1)
        rise = jnp.zeros((leaves, prank), F32)
        for i in range(leaves):
            rise = jnp.where(row == i, full[:, coefs + i * prank : coefs + (i + 1) * prank], rise)
        rise = rise + jnp.where(
            even, pltpu.roll(rise, leaves - 1, 0), pltpu.roll(rise, 1, 0)
        )
        own_ct[step, 0:leaves, :] = dup
        own_ct[step, leaves : 2 * leaves, :] = rise
        send(step, ct_copy)
        if early is not None:
            early()
        acc = 0.5 * field
        for i in range(leaves):
            acc = acc + jnp.where(row_w == i, nn(xb, near_t[i, 0]), 0.0)
        zero = jnp.zeros((leaves, LANES), F32)
        xs = pick_x(0, own_x.at[step], [[zero] * halves] * (n_near - 1))
        far, top = pick_ct(0, own_ct.at[step], [zero] * far_tiles, [zero] * n_top)
        receive(step, x_copy, 0)
        xs = pick_x(1, halo_x.at[step, 0], xs)
        receive(step, ct_copy, 0)
        far, top = pick_ct(1, halo_ct.at[step, 0], far, top)
        receive(step, x_copy, 1)
        xs = pick_x(2, halo_x.at[step, 1], xs)
        xs = [jnp.concatenate(x, 1).astype(BF16) for x in xs]

        def near_rows(acc, lo, hi):
            for i in range(lo, hi):
                r = nn(xs[0], near_t[i, 1])
                for k in range(2, n_near):
                    r = r + nn(xs[k - 1], near_t[i, k])
                acc = acc + jnp.where(row_w == i, r, 0.0)
            return acc

        acc = near_rows(acc, 0, leaves // 2)
        receive(step, ct_copy, 1)
        far, top = pick_ct(2, halo_ct.at[step, 1], far, top)
        lhs = jnp.concatenate(far + top, 1).astype(BF16)
        g = jnp.where(diag, nn(lhs, g_w[...]), 0.0).astype(BF16)
        acc = near_rows(acc, leaves // 2, leaves)
        return acc + nn(g, lb[...])

    def body(step, early):
        root = roots[0:1, 0:1]
        for s in range(1, steps):
            root = jnp.where(step == s, roots[0:1, s : s + 1], root)
        inverse = 1.0 / root
        prod = prod_buf[...]
        z = z_buf[...] + prod * inverse
        z_buf[...] = z
        last = step == steps - 1
        field = jnp.where(last, z, prod)
        image = apply(step, field, early)
        prod_buf[...] = jnp.where(last, image, prod - image * inverse)

    body(0, prepare)

    def loop(step, carry):
        body(step, None)
        return carry

    lax.fori_loop(1, steps, loop, 0)

    w = prod_buf[...]
    w_buf[...] = w
    proj = jnp.zeros((count, LANES), F32)
    for c in range(chunks):
        i, h = c // halves, c % halves
        proj = proj + bas[c * count : (c + 1) * count, :] * side_tile(w_buf, i, h * LANES)
    hcol = jnp.sum(proj, 1, keepdims=True)
    ww = jnp.sum(jnp.sum(w * w, 1, keepdims=True), 0, keepdims=True)
    at_h = count * count
    lane_c = iota((count, LANES), 1)
    row_c = iota((count, LANES), 0)
    lane1 = iota((1, LANES), 1)
    hsum = jnp.sum(jnp.where(lane_c == row_c + at_h, hcol, 0.0), 0, keepdims=True)
    slots[me] = gram_row[...] + hsum + jnp.where(lane1 == at_h + count, ww, 0.0)

    for target in others():
        pltpu.make_async_remote_copy(
            src_ref=slots.at[me],
            dst_ref=slots.at[me],
            send_sem=red_sem.at[0],
            recv_sem=red_sem.at[1],
            device_id=target,
            device_id_type=MESH,
        ).start()
    rest = pltpu.make_async_remote_copy(
        src_ref=slots.at[pl.ds(0, n_dev - 1)],
        dst_ref=slots.at[pl.ds(0, n_dev - 1)],
        send_sem=red_sem.at[0],
        recv_sem=red_sem.at[1],
        device_id=place(fast),
        device_id_type=MESH,
    )
    rest.wait_recv()
    total = jnp.sum(slots[...], 0) * (1.0 / (leaves * width * n_dev))
    hrow = jnp.where(lane1 < count, pltpu.roll(total, LANES - at_h, 1), 0.0)
    hcol = jnp.sum(jnp.where(lane_c == row_c, hrow, 0.0), 1, keepdims=True)
    gram = pltpu.roll(
        jnp.broadcast_to(total, (count, LANES)),
        LANES - count * (count - 1),
        1,
        stride=count,
        stride_axis=0,
    )
    quad = jnp.sum(hcol * (gram * hrow), 0, keepdims=True) - 2.0 * hrow * hrow
    quad = quad + jnp.where(lane1 == at_h + count, total, 0.0)
    squared = jnp.maximum(jnp.sum(quad, 1, keepdims=True), 0.0)
    beta = jnp.sqrt(squared + 1e-06)
    inverse = 1.0 / beta
    hess[...] = jnp.where(lane1 == count, beta, hrow)[:, 0 : count + 1]
    for h in range(halves):
        fit = jnp.zeros((leaves, LANES), F32)
        for j in range(count):
            vec = bas[pl.ds(j + count * h, leaves, stride=count * halves), :]
            fit = fit + hcol[j : j + 1, :] * vec
        part = w[:, h * LANES : (h + 1) * LANES]
        out[pl.ds(h, leaves, stride=halves), :] = (part - fit) * inverse
    rest.wait_send()

    def drain(step, carry):
        for make in (x_copy, ct_copy):
            make(step, 0).wait_send()

            @pl.when(has_slow)
            def _():
                make(step, 1).wait_send()

        return carry

    lax.fori_loop(0, steps, drain, 0)


def make_body(n_grp, n_leaf):
    def body(
        basis,
        roots,
        near_blocks,
        near_ids,
        leaf_basis,
        far_coupling,
        far_ids,
        transfer,
        top_coupling,
        top_ids,
    ):
        leaves, rank, width = leaf_basis.shape
        prank = transfer.shape[2]
        count = basis.shape[0]
        steps = roots.shape[0]
        n_near, n_far, n_top = near_ids.shape[1], far_ids.shape[1], top_ids.shape[1]
        n_dev = n_grp * n_leaf
        coefs = leaves * rank
        far_tiles = n_far * rank // LANES
        chunks = leaves * width // LANES
        vmem = pl.BlockSpec(memory_space=pltpu.VMEM)
        hbm = pl.BlockSpec(memory_space=pl.ANY)
        lb = leaf_basis.reshape(coefs, width)
        tr = transfer.reshape(coefs, prank)
        out, hess = pl.pallas_call(
            functools.partial(kernel, n_grp, n_leaf),
            out_shape=(
                jax.ShapeDtypeStruct((chunks, LANES), F32),
                jax.ShapeDtypeStruct((1, count + 1), F32),
            ),
            in_specs=[hbm] * 10,
            out_specs=(vmem, vmem),
            scratch_shapes=[
                pltpu.VMEM((chunks * count, LANES), F32),
                pltpu.VMEM((1, steps), F32),
                pltpu.VMEM(near_blocks.shape, BF16),
                pltpu.VMEM(near_blocks.shape, BF16),
                pltpu.VMEM(near_ids.shape, jnp.int32),
                pltpu.VMEM(lb.shape, BF16),
                pltpu.VMEM((width, coefs + leaves * prank), BF16),
                pltpu.VMEM(far_coupling.shape, BF16),
                pltpu.VMEM((coefs, n_far * rank), BF16),
                pltpu.VMEM(far_ids.shape, jnp.int32),
                pltpu.VMEM(tr.shape, BF16),
                pltpu.VMEM(top_coupling.shape, BF16),
                pltpu.VMEM(top_ids.shape, jnp.int32),
                pltpu.VMEM((n_far * rank + n_top * prank, coefs), BF16),
                pltpu.VMEM((3, n_near - 1, leaves, LANES), jnp.int32),
                pltpu.VMEM((3, far_tiles, leaves, LANES), jnp.int32),
                pltpu.VMEM((3, n_top, leaves, LANES), jnp.int32),
                pltpu.VMEM((steps, leaves, width), F32),
                pltpu.VMEM((steps, 2 * leaves, LANES), F32),
                pltpu.VMEM((steps, 2, leaves, width), F32),
                pltpu.VMEM((steps, 2, 2 * leaves, LANES), F32),
                pltpu.VMEM((leaves, width), F32),
                pltpu.VMEM((leaves, width), F32),
                pltpu.VMEM((leaves, width), F32),
                pltpu.VMEM((1, LANES), F32),
                pltpu.VMEM((n_dev, 1, LANES), F32),
                pltpu.SemaphoreType.DMA((9,)),
                pltpu.SemaphoreType.DMA((leaves,)),
                pltpu.SemaphoreType.DMA((steps, 2, 2)),
                pltpu.SemaphoreType.DMA((steps, 2, 2)),
                pltpu.SemaphoreType.DMA((2,)),
            ],
            compiler_params=pltpu.CompilerParams(
                collective_id=0, has_side_effects=True, vmem_limit_bytes=67043328
            ),
        )(
            basis,
            roots.reshape(1, steps),
            near_blocks,
            near_ids,
            lb,
            far_coupling,
            far_ids,
            tr,
            top_coupling,
            top_ids,
        )
        return out.reshape(leaves * width), hess.reshape(count + 1)

    return body


def solution(mesh):
    both = ("grp", "leaf")
    return jax.shard_map(
        make_body(mesh.shape["grp"], mesh.shape["leaf"]),
        mesh=mesh,
        in_specs=(
            P(None, both),
            P(),
            P(both, None, None, None),
            P(both, None),
            P(both, None, None),
            P(both, None, None, None),
            P(both, None),
            P(both, None, None),
            P(both, None, None, None),
            P(both, None),
        ),
        out_specs=(P(both), P()),
        check_vma=False,
    )
```

time: 58.4 us -> 43 us (0.74)
  Pallas kernels: 48.4 us -> 39.7 us
  local copies, waits for them, and re-layouts: 8.95 us -> 2.43 us
    pallas_call x1, Pallas kernels: 48.4 us -> 39.7 us  [body(): pl.pallas_call(functools.partial(kernel, n_grp, n_leaf), out_shape=(jax.S...]
    unnamed x20 -> x2, local copies, waits for them, and re-layouts: 8.95 us -> 2.43 us
where the time goes in v1:
time: 43 us; the launch traced here: 42.8 us
  Pallas kernels  39.7 us (92%)
  local copies, waits for them, and re-layouts  2.43 us (6%)
  between operations  0.64 us (1%)
    pallas_call x1, Pallas kernels, body(): pl.pallas_call(functools.partial(kernel, n_grp, n_leaf), out_shape=(jax.S...  39.7 us
    unnamed x2, local copies, waits for them, and re-layouts  2.43 us

profile of v1, /device:TPU:0, one launch (start us, length us, event | category | flops | bytes accessed | tf_op | source)
XLA Modules:
  0.0 42.8 jit_solution(16440993634340656308)
XLA Ops:
  0.6 39.7 %shard_map.113 = (f32[16,128]{1,0:T(8,128)}, f32[1,9]{1,0:T(1,128)}) custom-call(f32[8,2048]{1,0:T(8,128)} %basis_hbm.1, f32[1,5]{1,0:T(1,128)} %bitcast.8, bf16[8,6,256,256]{3,2,1,0:T(8,128)(2,1)} %near_hbm.1, s32[8,6]{1,0:T(8,128)} %near_ids_hbm.1, bf16[512,256]{1,0:T(8,128)(2,1)} %bitcast.5, bf16[8,8,64,64]{3,2,1,0:T(8,128)(2,1)} %fc_hbm.1, ...), custom_call_target="tpu_custom_call" | custom-call | tf_op jit(solution)/shard_map/pallas_call | solution.py:473
  40.3 1.3 %copy.14 = f32[2048]{0:T(1024)} copy(f32[2048]{0:T(1024)} %bitcast.7) | data formatting | bytes 16384
  41.6 1.1 %copy.15 = f32[9]{0:T(128)} copy(f32[9]{0:T(128)} %bitcast.9) | data formatting | bytes 72

commit v2 on v1

--- a/solution.py
+++ b/solution.py
@@ -71,8 +71,10 @@
     send_sem,
     recv_sem,
     red_sem,
+    ready_sem,
 ):
     n_dev = n_grp * n_leaf
+    rounds = ready_sem.shape[0]
     leaves, n_near, width, _ = near.shape
     n_far, rank = fc.shape[1], fc.shape[2]
     n_top, prank = tc.shape[1], tc.shape[2]
@@ -132,8 +134,25 @@
         pltpu.make_async_copy(near_hbm.at[i], near.at[i], near_sem.at[i]).start()
 
     barrier = pltpu.get_barrier_semaphore()
-    for target in others():
-        pl.semaphore_signal(barrier, inc=1, device_id=target, device_id_type=MESH)
+
+    def around(distance, call):
+        for other in (me - distance, me + distance):
+
+            @pl.when(jnp.logical_and(other >= 0, other < n_dev))
+            def _():
+                call(other)
+
+    def signal(sem, distance):
+        def one(other):
+            pl.semaphore_signal(sem, inc=1, device_id=place(other), device_id_type=MESH)
+
+        around(distance, one)
+
+    def await_signals(sem, distance):
+        peers = jnp.where(me >= distance, 1, 0) + jnp.where(me + distance < n_dev, 1, 0)
+        pl.semaphore_wait(sem, peers)
+
+    signal(barrier, 1)
 
     row = iota((leaves, LANES), 0)
     lane = iota((leaves, LANES), 1)
@@ -190,7 +209,7 @@
         block = nn(lb_t[:, i * rank : (i + 1) * rank], tr[i * rank : (i + 1) * rank, :])
         up_w[:, coefs + i * prank : coefs + (i + 1) * prank] = block.astype(BF16)
 
-    pl.semaphore_wait(barrier, n_dev - 1)
+    await_signals(barrier, 1)
 
     def x_copy(step, side):
         return pltpu.make_async_remote_copy(
@@ -301,7 +320,14 @@
     diag = iota((leaves, coefs), 0) == iota((leaves, coefs), 1) // rank
     row_w = iota((leaves, width), 0)
 
-    def apply(step, field, early):
+    def greet(step, distance):
+        @pl.when(step >= 2)
+        def _():
+            await_signals(ready_sem.at[step - 1], distance // 2)
+
+        signal(ready_sem.at[step], distance)
+
+    def apply(step, field, early, distance):
         own_x[step] = field
         send(step, x_copy)
         xb = field.astype(BF16)
@@ -322,6 +348,8 @@
         send(step, ct_copy)
         if early is not None:
             early()
+        else:
+            greet(step, distance)
         acc = 0.5 * field
         for i in range(leaves):
             acc = acc + jnp.where(row_w == i, nn(xb, near_t[i, 0]), 0.0)
@@ -352,7 +380,7 @@
         acc = near_rows(acc, leaves // 2, leaves)
         return acc + nn(g, lb[...])
 
-    def body(step, early):
+    def body(step, early, distance):
         root = roots[0:1, 0:1]
         for s in range(1, steps):
             root = jnp.where(step == s, roots[0:1, s : s + 1], root)
@@ -362,16 +390,20 @@
         z_buf[...] = z
         last = step == steps - 1
         field = jnp.where(last, z, prod)
-        image = apply(step, field, early)
+        image = apply(step, field, early, distance)
         prod_buf[...] = jnp.where(last, image, prod - image * inverse)
 
-    body(0, prepare)
-
-    def loop(step, carry):
-        body(step, None)
-        return carry
-
-    lax.fori_loop(1, steps, loop, 0)
+    body(0, prepare, 1)
+
+    def loop(step, distance):
+        body(step, None, distance)
+        return distance * 2
+
+    lax.fori_loop(1, steps, loop, 2)
+    await_signals(ready_sem.at[steps - 1], 2 ** (steps - 1))
+    for r in range(steps, rounds):
+        signal(ready_sem.at[r], 2**r)
+        await_signals(ready_sem.at[r], 2**r)
 
     w = prod_buf[...]
     w_buf[...] = w
@@ -510,21 +542,27 @@
                 pltpu.SemaphoreType.DMA((steps, 2, 2)),
                 pltpu.SemaphoreType.DMA((steps, 2, 2)),
                 pltpu.SemaphoreType.DMA((2,)),
+                pltpu.SemaphoreType.REGULAR((max(steps, (n_dev - 1).bit_length()),)),
             ],
             compiler_params=pltpu.CompilerParams(
-                collective_id=0, has_side_effects=True, vmem_limit_bytes=67043328
+                collective_id=0, has_side_effects=True, vmem_limit_bytes=48 * 1024 * 1024
             ),
         )(
-            basis,
-            roots.reshape(1, steps),
-            near_blocks,
-            near_ids,
-            lb,
-            far_coupling,
-            far_ids,
-            tr,
-            top_coupling,
-            top_ids,
+            *(
+                pltpu.with_memory_space_constraint(operand, pltpu.HBM)
+                for operand in (
+                    basis,
+                    roots.reshape(1, steps),
+                    near_blocks,
+                    near_ids,
+                    lb,
+                    far_coupling,
+                    far_ids,
+                    tr,
+                    top_coupling,
+                    top_ids,
+                )
+            )
         )
         return out.reshape(leaves * width), hess.reshape(count + 1)
 

time: 43 us -> 41 us (0.953)
  local copies, waits for them, and re-layouts: 2.43 us -> 1.11 us
  Pallas kernels: 39.7 us -> 39.1 us
    unnamed x2, local copies, waits for them, and re-layouts: 2.43 us -> 1.11 us
    pallas_call x1, Pallas kernels: 39.7 us -> 39.1 us  [body(): pl.pallas_call(functools.partial(kernel, n_grp, n_leaf), out_shape=(jax.S...]
where the time goes in v2:
time: 41 us; the launch traced here: 40.8 us
  Pallas kernels  39.1 us (95%)
  local copies, waits for them, and re-layouts  1.11 us (3%)
  between operations  0.64 us (2%)
    pallas_call x1, Pallas kernels, body(): pl.pallas_call(functools.partial(kernel, n_grp, n_leaf), out_shape=(jax.S...  39.1 us
    unnamed x2, local copies, waits for them, and re-layouts  1.11 us

profile of v2, /device:TPU:0, one launch (start us, length us, event | category | flops | bytes accessed | tf_op | source)
XLA Modules:
  0.0 40.8 jit_solution(173492888568832478)
XLA Ops:
  0.6 39.1 %shard_map.113 = (f32[16,128]{1,0:T(8,128)S(1)}, f32[1,9]{1,0:T(1,128)S(1)}) custom-call(f32[8,2048]{1,0:T(8,128)} %basis_hbm.1, f32[1,5]{1,0:T(1,128)} %bitcast.9, bf16[8,6,256,256]{3,2,1,0:T(8,128)(2,1)} %near_hbm.1, s32[8,6]{1,0:T(8,128)} %near_ids_hbm.1, bf16[512,256]{1,0:T(8,128)(2,1)} %bitcast.7, bf16[8,8,64,64]{3,2,1,0:T(8,128)(2,1)} %fc_hbm.1, ...), custom_call_target="tpu_custom_call" | custom-call | tf_op jit(solution)/shard_map/pallas_call | solution.py:505
  39.7 0.6 %copy.14 = f32[2048]{0:T(1024)} copy(f32[2048]{0:T(1024)S(1)} %bitcast.5) | data formatting | bytes 16384
  40.3 0.5 %copy.15 = f32[9]{0:T(128)} copy(f32[9]{0:T(128)S(1)} %bitcast.6) | data formatting | bytes 72

commit v3 on v2

--- a/solution.py
+++ b/solution.py
@@ -202,12 +202,8 @@
     z_buf[...] = jnp.zeros_like(z_buf)
 
     lb_copy.wait()
-    lb_t = lb[...].T
-    up_w[:, 0:coefs] = lb_t
+    up_w[...] = lb[...].T
     tr_copy.wait()
-    for i in range(leaves):
-        block = nn(lb_t[:, i * rank : (i + 1) * rank], tr[i * rank : (i + 1) * rank, :])
-        up_w[:, coefs + i * prank : coefs + (i + 1) * prank] = block.astype(BF16)
 
     await_signals(barrier, 1)
 
@@ -271,30 +267,35 @@
         return far, top
 
     def prepare():
-        def turn(i, carry):
-            pltpu.make_async_copy(near_hbm.at[i], near.at[i], near_sem.at[i]).wait()
-            for k in range(n_near):
-                near_t[i, k] = near[i, k].T
-            return carry
-
-        lax.fori_loop(0, leaves, turn, 0)
+        base = n_far * rank
         fc_copy.wait()
-        for k in range(n_far):
-            for i in range(leaves):
-                fcc[i * rank : (i + 1) * rank, k * rank : (k + 1) * rank] = fc[i, k]
-        g_w[0 : n_far * rank, :] = fcc[...].T
         tc_copy.wait()
-        base = n_far * rank
-
-        def fold(k, carry):
+
+        def fold(k):
             start = pl.multiple_of(base + k * prank, prank)
             for p in range(parents):
                 pair = tr[p * 2 * rank : (p + 1) * 2 * rank, :]
                 block = nn(pair, tc[p, k]).astype(BF16).T
                 g_w[pl.ds(start, prank), p * 2 * rank : (p + 1) * 2 * rank] = block
+
+        def turn(i, carry):
+            pltpu.make_async_copy(near_hbm.at[i], near.at[i], near_sem.at[i]).wait()
+            start = pl.multiple_of(i * rank, rank)
+            for k in range(n_far):
+                fcc[pl.ds(start, rank), k * rank : (k + 1) * rank] = fc[i, k]
+            if n_top == leaves:
+                fold(i)
+            for k in range(1, n_near):
+                near_t[i, k - 1] = near[i, k].T
             return carry
 
-        lax.fori_loop(0, n_top, fold, 0)
+        lax.fori_loop(0, leaves, turn, 0)
+        if n_top != leaves:
+            for k in range(n_top):
+                fold(k)
+        g_w[0:base, :] = fcc[...].T
+
+    def make_gram():
         flat = jnp.concatenate(
             [bas[c * count : (c + 1) * count, :] for c in range(chunks)], 1
         )
@@ -326,20 +327,18 @@
             await_signals(ready_sem.at[step - 1], distance // 2)
 
         signal(ready_sem.at[step], distance)
+        pl.when(step == 1)(make_gram)
 
     def apply(step, field, early, distance):
         own_x[step] = field
         send(step, x_copy)
         xb = field.astype(BF16)
-        full = nn(xb, up_w[...])
-        masked = jnp.where(diag, full[:, 0:coefs], 0.0)
+        masked = jnp.where(diag, nn(xb, up_w[...]), 0.0)
         part = masked[:, 0:LANES]
         for v in range(1, coefs // LANES):
             part = part + masked[:, v * LANES : (v + 1) * LANES]
         dup = part + pltpu.roll(part, rank, 1)
-        rise = jnp.zeros((leaves, prank), F32)
-        for i in range(leaves):
-            rise = jnp.where(row == i, full[:, coefs + i * prank : coefs + (i + 1) * prank], rise)
+        rise = nn(masked.astype(BF16), tr[...])
         rise = rise + jnp.where(
             even, pltpu.roll(rise, leaves - 1, 0), pltpu.roll(rise, 1, 0)
         )
@@ -352,7 +351,7 @@
             greet(step, distance)
         acc = 0.5 * field
         for i in range(leaves):
-            acc = acc + jnp.where(row_w == i, nn(xb, near_t[i, 0]), 0.0)
+            acc = acc + jnp.where(row_w == i, nt(xb, near[i, 0]), 0.0)
         zero = jnp.zeros((leaves, LANES), F32)
         xs = pick_x(0, own_x.at[step], [[zero] * halves] * (n_near - 1))
         far, top = pick_ct(0, own_ct.at[step], [zero] * far_tiles, [zero] * n_top)
@@ -366,9 +365,9 @@
 
         def near_rows(acc, lo, hi):
             for i in range(lo, hi):
-                r = nn(xs[0], near_t[i, 1])
-                for k in range(2, n_near):
-                    r = r + nn(xs[k - 1], near_t[i, k])
+                r = nn(xs[0], near_t[i, 0])
+                for k in range(1, n_near - 1):
+                    r = r + nn(xs[k], near_t[i, k])
                 acc = acc + jnp.where(row_w == i, r, 0.0)
             return acc
 
@@ -437,6 +436,17 @@
         device_id=place(fast),
         device_id_type=MESH,
     )
+    def drain(step, carry):
+        for make in (x_copy, ct_copy):
+            make(step, 0).wait_send()
+
+            @pl.when(has_slow)
+            def _():
+                make(step, 1).wait_send()
+
+        return carry
+
+    lax.fori_loop(0, steps, drain, 0)
     rest.wait_recv()
     total = jnp.sum(slots[...], 0) * (1.0 / (leaves * width * n_dev))
     hrow = jnp.where(lane1 < count, pltpu.roll(total, LANES - at_h, 1), 0.0)
@@ -462,18 +472,6 @@
         part = w[:, h * LANES : (h + 1) * LANES]
         out[pl.ds(h, leaves, stride=halves), :] = (part - fit) * inverse
     rest.wait_send()
-
-    def drain(step, carry):
-        for make in (x_copy, ct_copy):
-            make(step, 0).wait_send()
-
-            @pl.when(has_slow)
-            def _():
-                make(step, 1).wait_send()
-
-        return carry
-
-    lax.fori_loop(0, steps, drain, 0)
 
 
 def make_body(n_grp, n_leaf):
@@ -514,10 +512,10 @@
                 pltpu.VMEM((chunks * count, LANES), F32),
                 pltpu.VMEM((1, steps), F32),
                 pltpu.VMEM(near_blocks.shape, BF16),
-                pltpu.VMEM(near_blocks.shape, BF16),
+                pltpu.VMEM((leaves, n_near - 1, width, width), BF16),
                 pltpu.VMEM(near_ids.shape, jnp.int32),
                 pltpu.VMEM(lb.shape, BF16),
-                pltpu.VMEM((width, coefs + leaves * prank), BF16),
+                pltpu.VMEM((width, coefs), BF16),
                 pltpu.VMEM(far_coupling.shape, BF16),
                 pltpu.VMEM((coefs, n_far * rank), BF16),
                 pltpu.VMEM(far_ids.shape, jnp.int32),

time: 41 us -> 39.7 us (0.968)
  Pallas kernels: 39.1 us -> 37.8 us
    pallas_call x1, Pallas kernels: 39.1 us -> 37.8 us  [body(): pl.pallas_call(functools.partial(kernel, n_grp, n_leaf), out_shape=(jax.S...]
where the time goes in v3:
time: 39.7 us; the launch traced here: 39.6 us
  Pallas kernels  37.8 us (95%)
  local copies, waits for them, and re-layouts  1.11 us (3%)
  between operations  0.64 us (2%)
    pallas_call x1, Pallas kernels, body(): pl.pallas_call(functools.partial(kernel, n_grp, n_leaf), out_shape=(jax.S...  37.8 us
    unnamed x2, local copies, waits for them, and re-layouts  1.11 us

profile of v3, /device:TPU:0, one launch (start us, length us, event | category | flops | bytes accessed | tf_op | source)
XLA Modules:
  0.0 39.6 jit_solution(17144675353155586893)
XLA Ops:
  0.6 37.8 %shard_map.113 = (f32[16,128]{1,0:T(8,128)S(1)}, f32[1,9]{1,0:T(1,128)S(1)}) custom-call(f32[8,2048]{1,0:T(8,128)} %basis_hbm.1, f32[1,5]{1,0:T(1,128)} %bitcast.9, bf16[8,6,256,256]{3,2,1,0:T(8,128)(2,1)} %near_hbm.1, s32[8,6]{1,0:T(8,128)} %near_ids_hbm.1, bf16[512,256]{1,0:T(8,128)(2,1)} %bitcast.7, bf16[8,8,64,64]{3,2,1,0:T(8,128)(2,1)} %fc_hbm.1, ...), custom_call_target="tpu_custom_call" | custom-call | tf_op jit(solution)/shard_map/pallas_call | solution.py:503
  38.5 0.6 %copy.14 = f32[2048]{0:T(1024)} copy(f32[2048]{0:T(1024)S(1)} %bitcast.5) | data formatting | bytes 16384
  39.1 0.5 %copy.15 = f32[9]{0:T(128)} copy(f32[9]{0:T(128)S(1)} %bitcast.6) | data formatting | bytes 72

commit v4 on v3

--- a/solution.py
+++ b/solution.py
@@ -44,6 +44,7 @@
     roots,
     near,
     near_t,
+    near_f,
     near_ids,
     lb,
     up_w,
@@ -54,6 +55,8 @@
     tc,
     top_ids,
     g_w,
+    top_w,
+    tr_t,
     near_ix,
     far_ix,
     top_ix,
@@ -75,12 +78,14 @@
 ):
     n_dev = n_grp * n_leaf
     rounds = ready_sem.shape[0]
+    n_mxu = near_t.shape[0]
     leaves, n_near, width, _ = near.shape
     n_far, rank = fc.shape[1], fc.shape[2]
     n_top, prank = tc.shape[1], tc.shape[2]
     parents = tc.shape[0]
     count = basis_hbm.shape[0]
     steps = roots.shape[1]
+    mid = (n_mxu + leaves) // 2
     coefs = leaves * rank
     halves = width // LANES
     chunks = leaves * halves
@@ -96,12 +101,26 @@
     slow = me - 1 + 2 * odd
     has_slow = jnp.logical_and(slow >= 0, slow < n_dev)
 
-    def others():
-        for dg in range(n_grp):
-            g = lax.rem(mg + dg, n_grp)
-            for dl in range(n_leaf):
-                if dg or dl:
-                    yield (g, lax.rem(ml + dl, n_leaf))
+    barrier = pltpu.get_barrier_semaphore()
+
+    def around(distance, call):
+        for other in (me - distance, me + distance):
+
+            @pl.when(jnp.logical_and(other >= 0, other < n_dev))
+            def _():
+                call(other)
+
+    def signal(sem, distance):
+        def one(other):
+            pl.semaphore_signal(sem, inc=1, device_id=place(other), device_id_type=MESH)
+
+        around(distance, one)
+
+    def await_signals(sem, distance):
+        peers = jnp.where(me >= distance, 1, 0) + jnp.where(me + distance < n_dev, 1, 0)
+        pl.semaphore_wait(sem, peers)
+
+    signal(barrier, 1)
 
     first = [
         pltpu.make_async_copy(
@@ -133,26 +152,6 @@
     for i in range(leaves):
         pltpu.make_async_copy(near_hbm.at[i], near.at[i], near_sem.at[i]).start()
 
-    barrier = pltpu.get_barrier_semaphore()
-
-    def around(distance, call):
-        for other in (me - distance, me + distance):
-
-            @pl.when(jnp.logical_and(other >= 0, other < n_dev))
-            def _():
-                call(other)
-
-    def signal(sem, distance):
-        def one(other):
-            pl.semaphore_signal(sem, inc=1, device_id=place(other), device_id_type=MESH)
-
-        around(distance, one)
-
-    def await_signals(sem, distance):
-        peers = jnp.where(me >= distance, 1, 0) + jnp.where(me + distance < n_dev, 1, 0)
-        pl.semaphore_wait(sem, peers)
-
-    signal(barrier, 1)
 
     row = iota((leaves, LANES), 0)
     lane = iota((leaves, LANES), 1)
@@ -267,33 +266,42 @@
         return far, top
 
     def prepare():
-        base = n_far * rank
         fc_copy.wait()
         tc_copy.wait()
 
         def fold(k):
-            start = pl.multiple_of(base + k * prank, prank)
+            start = pl.multiple_of(k * prank, prank)
             for p in range(parents):
-                pair = tr[p * 2 * rank : (p + 1) * 2 * rank, :]
-                block = nn(pair, tc[p, k]).astype(BF16).T
-                g_w[pl.ds(start, prank), p * 2 * rank : (p + 1) * 2 * rank] = block
-
-        def turn(i, carry):
-            pltpu.make_async_copy(near_hbm.at[i], near.at[i], near_sem.at[i]).wait()
+                top_w[pl.ds(start, prank), p * prank : (p + 1) * prank] = tc[p, k].T
+
+        def build(i):
             start = pl.multiple_of(i * rank, rank)
             for k in range(n_far):
                 fcc[pl.ds(start, rank), k * rank : (k + 1) * rank] = fc[i, k]
             if n_top == leaves:
                 fold(i)
+
+        def turn(i, carry):
+            pltpu.make_async_copy(near_hbm.at[i], near.at[i], near_sem.at[i]).wait()
+            build(i)
             for k in range(1, n_near):
                 near_t[i, k - 1] = near[i, k].T
             return carry
 
-        lax.fori_loop(0, leaves, turn, 0)
+        def widen(i, carry):
+            pltpu.make_async_copy(near_hbm.at[i], near.at[i], near_sem.at[i]).wait()
+            build(i)
+            for k in range(1, n_near):
+                near_f[i - n_mxu, k - 1] = near[i, k].astype(F32)
+            return carry
+
+        lax.fori_loop(0, n_mxu, turn, 0)
+        lax.fori_loop(n_mxu, leaves, widen, 0)
         if n_top != leaves:
             for k in range(n_top):
                 fold(k)
-        g_w[0:base, :] = fcc[...].T
+        g_w[...] = fcc[...].T
+        tr_t[...] = tr[...].T
 
     def make_gram():
         flat = jnp.concatenate(
@@ -362,21 +370,61 @@
         receive(step, x_copy, 1)
         xs = pick_x(2, halo_x.at[step, 1], xs)
         xs = [jnp.concatenate(x, 1).astype(BF16) for x in xs]
-
-        def near_rows(acc, lo, hi):
-            for i in range(lo, hi):
-                r = nn(xs[0], near_t[i, 0])
-                for k in range(1, n_near - 1):
-                    r = r + nn(xs[k], near_t[i, k])
-                acc = acc + jnp.where(row_w == i, r, 0.0)
+        rows = [x.astype(F32) for x in xs]
+
+        def vector_tiles(i):
+            return [
+                [jnp.broadcast_to(x[i : i + 1, h * LANES : (h + 1) * LANES], (leaves, LANES))
+                    for h in range(halves)]
+                for x in rows
+            ]
+
+        def vector_group(i, tiles, top):
+            r = None
+            for k in range(n_near - 1):
+                for h in range(halves):
+                    w = near_f[i - n_mxu, k, top : top + leaves, h * LANES : (h + 1) * LANES]
+                    r = w * tiles[k][h] if r is None else r + w * tiles[k][h]
+            return jnp.sum(r, 1, keepdims=True)
+
+        def near_part(acc, m_lo, m_hi, v_lo, v_hi):
+            groups = [(i, top) for i in range(v_lo, v_hi) for top in range(0, width, leaves)]
+            order = []
+            for i in range(m_lo, m_hi, 2):
+                pair = range(i, min(i + 2, m_hi))
+                order += [(m, k) for k in range(n_near - 1) for m in pair]
+            tiles = {i: vector_tiles(i) for i in range(v_lo, v_hi)}
+            parts = {}
+            sums = {}
+            done = 0
+            for n, (m, k) in enumerate(order):
+                dot = nn(xs[k], near_t[m, k])
+                sums[m] = sums[m] + dot if m in sums else dot
+                upto = len(groups) * (n + 1) // len(order)
+                for i, top in groups[done:upto]:
+                    o = top // LANES
+                    part = parts.get((i, o), jnp.zeros((leaves, LANES), F32))
+                    r = vector_group(i, tiles[i], top)
+                    parts[i, o] = jnp.where(lane == row + top % LANES, r, part)
+                done = upto
+            for m in sums:
+                acc = acc + jnp.where(row_w == m, sums[m], 0.0)
+            for i in range(v_lo, v_hi):
+                r = [jnp.sum(parts[i, o], 0, keepdims=True) for o in range(halves)]
+                acc = acc + jnp.where(row_w == i, jnp.concatenate(r, 1), 0.0)
             return acc
 
-        acc = near_rows(acc, 0, leaves // 2)
+        acc = near_part(acc, 0, n_mxu // 2, n_mxu, mid)
         receive(step, ct_copy, 1)
         far, top = pick_ct(2, halo_ct.at[step, 1], far, top)
-        lhs = jnp.concatenate(far + top, 1).astype(BF16)
-        g = jnp.where(diag, nn(lhs, g_w[...]), 0.0).astype(BF16)
-        acc = near_rows(acc, leaves // 2, leaves)
+        tops = nn(jnp.concatenate(top, 1).astype(BF16), top_w[...])
+        srow = tops[:, 0:prank]
+        for p in range(1, parents):
+            srow = jnp.where(row // 2 == p, tops[:, p * prank : (p + 1) * prank], srow)
+        leaf_sum = nn(jnp.concatenate(far, 1).astype(BF16), g_w[...])
+        down = nn(srow.astype(BF16), tr_t[...])
+        g = jnp.where(diag, leaf_sum + down, 0.0).astype(BF16)
+        acc = near_part(acc, n_mxu // 2, n_mxu, mid, leaves)
         return acc + nn(g, lb[...])
 
     def body(step, early, distance):
@@ -419,15 +467,20 @@
     hsum = jnp.sum(jnp.where(lane_c == row_c + at_h, hcol, 0.0), 0, keepdims=True)
     slots[me] = gram_row[...] + hsum + jnp.where(lane1 == at_h + count, ww, 0.0)
 
-    for target in others():
-        pltpu.make_async_remote_copy(
-            src_ref=slots.at[me],
-            dst_ref=slots.at[me],
-            send_sem=red_sem.at[0],
-            recv_sem=red_sem.at[1],
-            device_id=target,
-            device_id_type=MESH,
-        ).start()
+    for g in range(n_grp):
+        for l in range(n_leaf):
+
+            @pl.when(me != g * n_leaf + l)
+            def _():
+                pltpu.make_async_remote_copy(
+                    src_ref=slots.at[me],
+                    dst_ref=slots.at[me],
+                    send_sem=red_sem.at[0],
+                    recv_sem=red_sem.at[1],
+                    device_id=(g, l),
+                    device_id_type=MESH,
+                ).start()
+
     rest = pltpu.make_async_remote_copy(
         src_ref=slots.at[pl.ds(0, n_dev - 1)],
         dst_ref=slots.at[pl.ds(0, n_dev - 1)],
@@ -493,6 +546,7 @@
         steps = roots.shape[0]
         n_near, n_far, n_top = near_ids.shape[1], far_ids.shape[1], top_ids.shape[1]
         n_dev = n_grp * n_leaf
+        n_vec = leaves // 2
         coefs = leaves * rank
         far_tiles = n_far * rank // LANES
         chunks = leaves * width // LANES
@@ -512,7 +566,8 @@
                 pltpu.VMEM((chunks * count, LANES), F32),
                 pltpu.VMEM((1, steps), F32),
                 pltpu.VMEM(near_blocks.shape, BF16),
-                pltpu.VMEM((leaves, n_near - 1, width, width), BF16),
+                pltpu.VMEM((leaves - n_vec, n_near - 1, width, width), BF16),
+                pltpu.VMEM((n_vec, n_near - 1, width, width), F32),
                 pltpu.VMEM(near_ids.shape, jnp.int32),
                 pltpu.VMEM(lb.shape, BF16),
                 pltpu.VMEM((width, coefs), BF16),
@@ -522,7 +577,9 @@
                 pltpu.VMEM(tr.shape, BF16),
                 pltpu.VMEM(top_coupling.shape, BF16),
                 pltpu.VMEM(top_ids.shape, jnp.int32),
-                pltpu.VMEM((n_far * rank + n_top * prank, coefs), BF16),
+                pltpu.VMEM((n_far * rank, coefs), BF16),
+                pltpu.VMEM((n_top * prank, leaves // 2 * prank), BF16),
+                pltpu.VMEM((prank, coefs), BF16),
                 pltpu.VMEM((3, n_near - 1, leaves, LANES), jnp.int32),
                 pltpu.VMEM((3, far_tiles, leaves, LANES), jnp.int32),
                 pltpu.VMEM((3, n_top, leaves, LANES), jnp.int32),

time: 39.7 us -> 38.9 us (0.980)
  Pallas kernels: 37.8 us -> 37 us
    pallas_call x1, Pallas kernels: 37.8 us -> 37 us  [body(): pl.pallas_call(functools.partial(kernel, n_grp, n_leaf), out_shape=(jax.S...]
where the time goes in v4:
time: 38.9 us; the launch traced here: 38.8 us
  Pallas kernels  37 us (95%)
  local copies, waits for them, and re-layouts  1.11 us (3%)
  between operations  0.64 us (2%)
    pallas_call x1, Pallas kernels, body(): pl.pallas_call(functools.partial(kernel, n_grp, n_leaf), out_shape=(jax.S...  37 us
    unnamed x2, local copies, waits for them, and re-layouts  1.11 us

profile of v4, /device:TPU:0, one launch (start us, length us, event | category | flops | bytes accessed | tf_op | source)
XLA Modules:
  0.0 38.8 jit_solution(17023504033976893892)
XLA Ops:
  0.6 37.0 %shard_map.113 = (f32[16,128]{1,0:T(8,128)S(1)}, f32[1,9]{1,0:T(1,128)S(1)}) custom-call(f32[8,2048]{1,0:T(8,128)} %basis_hbm.1, f32[1,5]{1,0:T(1,128)} %bitcast.9, bf16[8,6,256,256]{3,2,1,0:T(8,128)(2,1)} %near_hbm.1, s32[8,6]{1,0:T(8,128)} %near_ids_hbm.1, bf16[512,256]{1,0:T(8,128)(2,1)} %bitcast.7, bf16[8,8,64,64]{3,2,1,0:T(8,128)(2,1)} %fc_hbm.1, ...), custom_call_target="tpu_custom_call" | custom-call | tf_op jit(solution)/shard_map/pallas_call | solution.py:557
  37.6 0.6 %copy.14 = f32[2048]{0:T(1024)} copy(f32[2048]{0:T(1024)S(1)} %bitcast.5) | data formatting | bytes 16384
  38.2 0.5 %copy.15 = f32[9]{0:T(128)} copy(f32[9]{0:T(128)S(1)} %bitcast.6) | data formatting | bytes 72

commit v5 on v4

--- a/solution.py
+++ b/solution.py
@@ -65,7 +65,6 @@
     halo_x,
     halo_ct,
     prod_buf,
-    z_buf,
     w_buf,
     gram_row,
     slots,
@@ -198,7 +197,6 @@
         prod_buf[:, h * LANES : (h + 1) * LANES] = bas[
             pl.ds(count - 1 + count * h, leaves, stride=count * halves), :
         ]
-    z_buf[...] = jnp.zeros_like(z_buf)
 
     lb_copy.wait()
     up_w[...] = lb[...].T
@@ -330,12 +328,12 @@
     row_w = iota((leaves, width), 0)
 
     def greet(step, distance):
-        @pl.when(step >= 2)
-        def _():
+        if step >= 2:
             await_signals(ready_sem.at[step - 1], distance // 2)
 
         signal(ready_sem.at[step], distance)
-        pl.when(step == 1)(make_gram)
+        if step == 1:
+            make_gram()
 
     def apply(step, field, early, distance):
         own_x[step] = field
@@ -427,32 +425,19 @@
         acc = near_part(acc, n_mxu // 2, n_mxu, mid, leaves)
         return acc + nn(g, lb[...])
 
-    def body(step, early, distance):
-        root = roots[0:1, 0:1]
-        for s in range(1, steps):
-            root = jnp.where(step == s, roots[0:1, s : s + 1], root)
-        inverse = 1.0 / root
-        prod = prod_buf[...]
-        z = z_buf[...] + prod * inverse
-        z_buf[...] = z
+    inverses = [1.0 / roots[0:1, s : s + 1] for s in range(steps)]
+    w = prod_buf[...]
+    z = jnp.zeros_like(w)
+    for step in range(steps):
+        z = z + w * inverses[step]
         last = step == steps - 1
-        field = jnp.where(last, z, prod)
-        image = apply(step, field, early, distance)
-        prod_buf[...] = jnp.where(last, image, prod - image * inverse)
-
-    body(0, prepare, 1)
-
-    def loop(step, distance):
-        body(step, None, distance)
-        return distance * 2
-
-    lax.fori_loop(1, steps, loop, 2)
+        image = apply(step, z if last else w, None if step else prepare, 2**step)
+        w = image if last else w - image * inverses[step]
     await_signals(ready_sem.at[steps - 1], 2 ** (steps - 1))
     for r in range(steps, rounds):
         signal(ready_sem.at[r], 2**r)
         await_signals(ready_sem.at[r], 2**r)
 
-    w = prod_buf[...]
     w_buf[...] = w
     proj = jnp.zeros((count, LANES), F32)
     for c in range(chunks):
@@ -589,7 +574,6 @@
                 pltpu.VMEM((steps, 2, 2 * leaves, LANES), F32),
                 pltpu.VMEM((leaves, width), F32),
                 pltpu.VMEM((leaves, width), F32),
-                pltpu.VMEM((leaves, width), F32),
                 pltpu.VMEM((1, LANES), F32),
                 pltpu.VMEM((n_dev, 1, LANES), F32),
                 pltpu.SemaphoreType.DMA((9,)),

time: 38.9 us -> 37.3 us (0.959)
  Pallas kernels: 37 us -> 35.4 us
    pallas_call x1, Pallas kernels: 37 us -> 35.4 us  [body(): pl.pallas_call(functools.partial(kernel, n_grp, n_leaf), out_shape=(jax.S...]
where the time goes in v5:
time: 37.3 us; the launch traced here: 37.2 us
  Pallas kernels  35.4 us (95%)
  local copies, waits for them, and re-layouts  1.11 us (3%)
  between operations  0.64 us (2%)
    pallas_call x1, Pallas kernels, body(): pl.pallas_call(functools.partial(kernel, n_grp, n_leaf), out_shape=(jax.S...  35.4 us
    unnamed x2, local copies, waits for them, and re-layouts  1.11 us

profile of v5, /device:TPU:0, one launch (start us, length us, event | category | flops | bytes accessed | tf_op | source)
XLA Modules:
  0.0 37.2 jit_solution(10559008125677842346)
XLA Ops:
  0.6 35.4 %shard_map.113 = (f32[16,128]{1,0:T(8,128)S(1)}, f32[1,9]{1,0:T(1,128)S(1)}) custom-call(f32[8,2048]{1,0:T(8,128)} %basis_hbm.1, f32[1,5]{1,0:T(1,128)} %bitcast.9, bf16[8,6,256,256]{3,2,1,0:T(8,128)(2,1)} %near_hbm.1, s32[8,6]{1,0:T(8,128)} %near_ids_hbm.1, bf16[512,256]{1,0:T(8,128)(2,1)} %bitcast.7, bf16[8,8,64,64]{3,2,1,0:T(8,128)(2,1)} %fc_hbm.1, ...), custom_call_target="tpu_custom_call" | custom-call | tf_op jit(solution)/shard_map/pallas_call | solution.py:542
  36.1 0.6 %copy.14 = f32[2048]{0:T(1024)} copy(f32[2048]{0:T(1024)S(1)} %bitcast.5) | data formatting | bytes 16384
  36.7 0.5 %copy.15 = f32[9]{0:T(128)} copy(f32[9]{0:T(128)S(1)} %bitcast.6) | data formatting | bytes 72
